TPU v7x, 32 devices: a whole 2x2x4 slice. The times are simulated.
32 devices in a mesh: section: 4 (over y, x), dp: 8 (over z, core).
Axes of the slice: x: 2, y: 2, z: 4, core: 2. Of those that a mesh axis runs over, the one named last changes fastest.
Arguments:
- latent: bfloat16 [2048, 1536], P('dp'), may hold values from -6 to 6
- target: bfloat16 [2048, 1536], P('dp'), may hold values from -6 to 6
- camera_of_token: int32 [2048], P('dp'), may hold values from 0 to 5
- timestep_indices: int32 [2], replicated, may hold values from 0 to 49
- camera_embedding_table: bfloat16 [6, 1536], replicated, may hold values from -3 to 3
- timestep_embedding_table: bfloat16 [50, 1536], replicated, may hold values from -2.5 to 2.5
- layer_norm_gain: float32 [4, 1536], P('section'), may hold values from 0.25 to 1.75
- frozen_weight: bfloat16 [4, 1536, 1536], P('section', 'dp'), may hold values from -0.15625 to 0.15625
- adapter_down_weight: bfloat16 [4, 64, 1536], P('section'), may hold values from -0.15625 to 0.15625
- adapter_up_weight: bfloat16 [4, 64, 1536], P('section'), may hold values from -0.75 to 0.75
Outputs:
- grad_down: float32 [4, 64, 1536], P('section', None, 'dp')
- grad_up: float32 [4, 64, 1536], P('section', None, 'dp')
Inputs may be any that keep to these rules, and one draw needn't show every extreme that they name: `timestep_indices`: indices of rows of timestep_embedding_table.
All inputs are finite; a program needn't handle non-finite values.
Results may differ from a plain program's by a relative error of at most 0.024.
Values may be sent and summed in bfloat16 or wider, within the bound.
A program may use at most 64 MiB of HBM per device.

v0:
```python
import math

import jax
import jax.numpy as jnp
from jax import lax
from jax.sharding import PartitionSpec as P

MICRO = 4


BLEND = 0.5
ADAPTER_SCALE = 0.5
EPSILON = 1e-06


def from_behind(block, axis, distance):
    devices = range(lax.axis_size(axis))
    route = [((i - distance) % len(devices), i) for i in devices]
    return lax.ppermute(block, axis, route)


def forward_layer_pass(
    hidden_state, layer_weight, down_weight_rows, up_weight_rows, gain_row, modulate_row
):
    hidden_float = hidden_state.astype(jnp.float32)
    inverse_rms = lax.rsqrt(jnp.mean(hidden_float * hidden_float, axis=-1, keepdims=True) + EPSILON)
    normalized_hidden = (hidden_float * inverse_rms * (gain_row * modulate_row)).astype(
        jnp.bfloat16
    )
    low_rank_hidden = lax.dot_general(
        normalized_hidden,
        down_weight_rows,
        (((1,), (1,)), ((), ())),
        preferred_element_type=jnp.float32,
    ).astype(jnp.bfloat16)
    preactivation = jnp.dot(
        normalized_hidden, layer_weight, preferred_element_type=jnp.float32
    ) + ADAPTER_SCALE * jnp.dot(low_rank_hidden, up_weight_rows, preferred_element_type=jnp.float32)
    output = (hidden_float + jax.nn.silu(preactivation)).astype(jnp.bfloat16)
    return (output, normalized_hidden, low_rank_hidden, preactivation)


def backward_layer_pass(
    hidden_state,
    normalized_hidden,
    low_rank_hidden,
    preactivation,
    output_gradient,
    layer_weight,
    down_weight_rows,
    up_weight_rows,
    gain_row,
    modulate_row,
):
    sigmoid_value = jax.nn.sigmoid(preactivation)
    preactivation_gradient = (
        output_gradient * sigmoid_value * (1.0 + preactivation * (1.0 - sigmoid_value))
    ).astype(jnp.bfloat16)
    low_rank_gradient = (
        ADAPTER_SCALE
        * lax.dot_general(
            preactivation_gradient,
            up_weight_rows,
            (((1,), (1,)), ((), ())),
            preferred_element_type=jnp.float32,
        )
    ).astype(jnp.bfloat16)
    norm_grad = lax.dot_general(
        preactivation_gradient,
        layer_weight,
        (((1,), (1,)), ((), ())),
        preferred_element_type=jnp.float32,
    ) + jnp.dot(low_rank_gradient, down_weight_rows, preferred_element_type=jnp.float32)
    up_gradient_term = ADAPTER_SCALE * lax.dot_general(
        low_rank_hidden,
        preactivation_gradient,
        (((0,), (0,)), ((), ())),
        preferred_element_type=jnp.float32,
    )
    down_gradient_term = lax.dot_general(
        low_rank_gradient,
        normalized_hidden,
        (((0,), (0,)), ((), ())),
        preferred_element_type=jnp.float32,
    )
    hidden_float = hidden_state.astype(jnp.float32)
    inverse_rms = lax.rsqrt(jnp.mean(hidden_float * hidden_float, axis=-1, keepdims=True) + EPSILON)
    scaled = hidden_float * inverse_rms
    scaled_grad = norm_grad * (gain_row * modulate_row)
    hidden_gradient = output_gradient + inverse_rms * (
        scaled_grad - scaled * jnp.mean(scaled_grad * scaled, axis=-1, keepdims=True)
    )
    return (hidden_gradient, down_gradient_term, up_gradient_term)


def pick_block(store, first_index, second_index):
    anchor = jnp.zeros((), jnp.int32)
    starts = (first_index, second_index) + (anchor,) * (store.ndim - 2)
    piece = lax.dynamic_slice(store, starts, (1, 1) + store.shape[2:])
    return piece[0, 0]


def place_block(store, value, first_index, second_index):
    anchor = jnp.zeros((), jnp.int32)
    starts = (first_index, second_index) + (anchor,) * (store.ndim - 2)
    return lax.dynamic_update_slice(store, value[None, None], starts)


def local(
    latent,
    target,
    camera_of_token,
    timestep_indices,
    camera_embedding_table,
    timestep_embedding_table,
    layer_norm_gain,
    frozen_weight,
    adapter_down_weight,
    adapter_up_weight,
):
    sections = lax.axis_size("section")
    position = lax.axis_index("section")
    layer_weight = lax.all_gather(frozen_weight[0], "dp", axis=0, tiled=True)
    down_weight_rows = adapter_down_weight[0]
    up_weight_rows = adapter_up_weight[0]
    gain_row = layer_norm_gain[0]
    feature_width = latent.shape[1]
    rank_width = down_weight_rows.shape[0]
    scale_factor = 1.0 / math.sqrt(latent.shape[0] * lax.axis_size("dp"))
    camera_rows = jnp.dot(
        jax.nn.one_hot(camera_of_token, camera_embedding_table.shape[0], dtype=jnp.bfloat16),
        camera_embedding_table,
        preferred_element_type=jnp.float32,
    )
    timestep_modulation = 1.0 + jnp.dot(
        jax.nn.one_hot(timestep_indices, timestep_embedding_table.shape[0], dtype=jnp.bfloat16),
        timestep_embedding_table,
        preferred_element_type=jnp.float32,
    )
    block_count = MICRO // 2
    block_rows = latent.shape[0] // block_count
    latent_blocks = latent.reshape(block_count, block_rows, feature_width)
    target_blocks = target.reshape(block_count, block_rows, feature_width)
    camera_blocks = camera_rows.reshape(block_count, block_rows, feature_width)
    is_first = position == 0
    is_last = position == sections - 1
    tick_total = 2 * sections + block_count - 1
    zero_index = jnp.zeros((), jnp.int32)

    def forward_tick(tick_index, carry):
        offset = tick_index - position
        round_index = (offset >= sections).astype(jnp.int32)
        block_index = offset - round_index * sections
        active = (offset >= 0) & (block_index < block_count)
        safe_block = jnp.clip(block_index, 0, block_count - 1)

        def forward_compute(current):
            (
                received,
                hidden_store,
                normed_store,
                low_store,
                pre_store,
                blend_store,
                adjoint_store,
            ) = current
            latent_block = lax.dynamic_index_in_dim(
                latent_blocks, safe_block, 0, keepdims=False
            ).astype(jnp.float32)
            camera_block = lax.dynamic_index_in_dim(camera_blocks, safe_block, 0, keepdims=False)
            target_block = lax.dynamic_index_in_dim(
                target_blocks, safe_block, 0, keepdims=False
            ).astype(jnp.float32)
            starting = jnp.where(round_index == 0, latent_block, received.astype(jnp.float32))
            first_hidden = (starting + camera_block).astype(jnp.bfloat16)
            hidden_state = jnp.where(is_first, first_hidden, received)
            modulate_row = jnp.where(
                round_index == 0, timestep_modulation[0], timestep_modulation[1]
            )
            output, normalized_hidden, low_rank_hidden, preactivation = forward_layer_pass(
                hidden_state, layer_weight, down_weight_rows, up_weight_rows, gain_row, modulate_row
            )
            hidden_store = place_block(hidden_store, hidden_state, round_index, safe_block)
            normed_store = place_block(normed_store, normalized_hidden, round_index, safe_block)
            low_store = place_block(low_store, low_rank_hidden, round_index, safe_block)
            pre_store = place_block(pre_store, preactivation, round_index, safe_block)
            previous_blend = lax.dynamic_index_in_dim(blend_store, safe_block, 0, keepdims=False)
            previous = jnp.where(round_index == 0, latent_block, previous_blend.astype(jnp.float32))
            blended = BLEND * (previous + output.astype(jnp.float32))
            blend_rounded = blended.astype(jnp.bfloat16)
            keep_blend = jnp.where(round_index == 0, blend_rounded, previous_blend)
            blend_store = lax.dynamic_update_slice(
                blend_store, keep_blend[None], (safe_block, zero_index, zero_index)
            )
            squashed = jnp.tanh(blended)
            adjoint = target_block * (1.0 - squashed * squashed) * scale_factor
            previous_adjoint = lax.dynamic_index_in_dim(
                adjoint_store, safe_block, 0, keepdims=False
            )
            keep_adjoint = jnp.where(round_index == 1, adjoint, previous_adjoint)
            adjoint_store = lax.dynamic_update_slice(
                adjoint_store, keep_adjoint[None], (safe_block, zero_index, zero_index)
            )
            outgoing = jnp.where(is_last, blend_rounded, output)
            return (
                outgoing,
                (hidden_store, normed_store, low_store, pre_store, blend_store, adjoint_store),
            )

        def forward_skip_block(current):
            return (jnp.zeros_like(current[0]), tuple(current[1:]))

        outgoing, stores = lax.cond(active, forward_compute, forward_skip_block, carry)
        incoming = from_behind(outgoing, "section", 1)
        return (incoming,) + tuple(stores)

    forward_start = (
        jnp.zeros((block_rows, feature_width), jnp.bfloat16),
        jnp.zeros((2, block_count, block_rows, feature_width), jnp.bfloat16),
        jnp.zeros((2, block_count, block_rows, feature_width), jnp.bfloat16),
        jnp.zeros((2, block_count, block_rows, rank_width), jnp.bfloat16),
        jnp.zeros((2, block_count, block_rows, feature_width), jnp.float32),
        jnp.zeros((block_count, block_rows, feature_width), jnp.bfloat16),
        jnp.zeros((block_count, block_rows, feature_width), jnp.float32),
    )
    forward_end = lax.fori_loop(0, tick_total, forward_tick, forward_start)
    hidden_store, normed_store, low_store, pre_store, blend_store, adjoint_store = forward_end[1:]
    back_position = sections - 1 - position

    def backward_tick(tick_index, carry):
        offset = tick_index - back_position
        round_back = (offset >= sections).astype(jnp.int32)
        block_index = offset - round_back * sections
        active = (offset >= 0) & (block_index < block_count)
        safe_block = jnp.clip(block_index, 0, block_count - 1)
        forward_round = 1 - round_back

        def backward_compute(current):
            received, down_sum, up_sum = current
            adjoint_block = lax.dynamic_index_in_dim(adjoint_store, safe_block, 0, keepdims=False)
            received_float = received.astype(jnp.float32)
            last_cotangent = jnp.where(
                round_back == 0,
                BLEND * adjoint_block,
                BLEND * (BLEND * adjoint_block + received_float),
            )
            output_gradient = jnp.where(is_last, last_cotangent, received_float)
            hidden_state = pick_block(hidden_store, forward_round, safe_block)
            normalized_hidden = pick_block(normed_store, forward_round, safe_block)
            low_rank_hidden = pick_block(low_store, forward_round, safe_block)
            preactivation = pick_block(pre_store, forward_round, safe_block)
            modulate_row = jnp.where(
                forward_round == 0, timestep_modulation[0], timestep_modulation[1]
            )
            hidden_gradient, down_gradient_term, up_gradient_term = backward_layer_pass(
                hidden_state,
                normalized_hidden,
                low_rank_hidden,
                preactivation,
                output_gradient,
                layer_weight,
                down_weight_rows,
                up_weight_rows,
                gain_row,
                modulate_row,
            )
            return (
                hidden_gradient.astype(jnp.bfloat16),
                down_sum + down_gradient_term,
                up_sum + up_gradient_term,
            )

        def backward_skip_block(current):
            return (jnp.zeros_like(current[0]), current[1], current[2])

        outgoing, down_sum, up_sum = lax.cond(active, backward_compute, backward_skip_block, carry)
        incoming = from_behind(outgoing, "section", -1)
        return (incoming, down_sum, up_sum)

    backward_start = (
        jnp.zeros((block_rows, feature_width), jnp.bfloat16),
        jnp.zeros((rank_width, feature_width), jnp.float32),
        jnp.zeros((rank_width, feature_width), jnp.float32),
    )
    backward_end = lax.fori_loop(0, tick_total, backward_tick, backward_start)
    down_part, up_part = (
        lax.psum_scatter(backward_end[1], "dp", scatter_dimension=1, tiled=True),
        lax.psum_scatter(backward_end[2], "dp", scatter_dimension=1, tiled=True),
    )
    return (down_part[None], up_part[None])


def solution(mesh):
    in_specs = (
        P("dp", None),
        P("dp", None),
        P("dp"),
        P(),
        P(),
        P(),
        P("section", None),
        P("section", "dp", None),
        P("section", None, None),
        P("section", None, None),
    )
    out_specs = (P("section", None, "dp"), P("section", None, "dp"))
    return jax.shard_map(local, mesh=mesh, in_specs=in_specs, out_specs=out_specs, check_vma=False)
```

profile of v0, /device:TPU:0, one launch (start us, length us, event | category | flops | bytes accessed | tf_op | source)
XLA Modules:
  0.0 546.5 jit_solution(1215283409359665392)
XLA Ops:
  11.9 51.6 %all-gather.3.cloned.1.call-done = bf16[1,1536,1536]{2,1,0:T(8,128)(2,1)} async-done(((bf16[1,192,1536]{2,1,0:T(8,128)(2,1)}), bf16[1,1536,1536]{2,1,0:T(8,128)(2,1)}) %all-gather.3.cloned.1.call-update) | async-done | bytes 4718608 | tf_op jit(solution)/shard_map/all_gather | solution.py:123
  69.1 208.6 %while.42 = (s32[]{:T(128)}, bf16[128,1536]{1,0:T(8,128)(2,1)S(1)}, bf16[2,2,128,1536]{3,2,1,0:T(8,128)(2,1)}, bf16[2,2,128,1536]{3,2,1,0:T(8,128)(2,1)}, bf16[2...) while((s32[]{:T(128)}, bf16[128,1536]{1,0:T(8,128)(2,1)S(1)}, ...), condition=%wide.region_4.5_spmd, body=%wide.region_0.4_spmd.sunk | while | flops 664349824 | bytes 28027136 | solution.py:226
  69.1 14.2 %conditional.4 = (bf16[128,1536]{1,0:T(8,128)(2,1)}, bf16[2,2,128,1536]{3,2,1,0:T(8,128)(2,1)}, bf16[2,2,128,1536]{3,2,1,0:T(8,128)(2,1)}, bf16[2,2,128,64]{2,3,...) conditional(s32[]{:T(128)} %convert_element_type.166, ...), branch_computations={%region_1.1_spmd, %region_2.3_spmd} | conditional | flops 664349824 | bytes 26453752 | solution.py:213
  83.4 12.4 %collective-permute-done = bf16[128,1536]{1,0:T(8,128)(2,1)S(1)} collective-permute-done((bf16[128,1536]{1,0:T(8,128)(2,1)}, bf16[128,1536]{1,0:T(8,128)(2,1)S(1)}, u32[]{:S(2)}, u32[]{:S(2)}) %collective-permute-start) | collective-permute-done | bytes 393248 | tf_op jit(solution)/shard_map/while/body/eval_jaxpr/ppermute | solution.py:19
  95.7 14.2 %conditional.4 = (bf16[128,1536]{1,0:T(8,128)(2,1)}, bf16[2,2,128,1536]{3,2,1,0:T(8,128)(2,1)}, bf16[2,2,128,1536]{3,2,1,0:T(8,128)(2,1)}, bf16[2,2,128,64]{2,3,...) conditional(s32[]{:T(128)} %convert_element_type.166, ...), branch_computations={%region_1.1_spmd, %region_2.3_spmd} | conditional | flops 664349824 | bytes 26453752 | solution.py:213
  110.0 11.5 %collective-permute-done = bf16[128,1536]{1,0:T(8,128)(2,1)S(1)} collective-permute-done((bf16[128,1536]{1,0:T(8,128)(2,1)}, bf16[128,1536]{1,0:T(8,128)(2,1)S(1)}, u32[]{:S(2)}, u32[]{:S(2)}) %collective-permute-start) | collective-permute-done | bytes 393248 | tf_op jit(solution)/shard_map/while/body/eval_jaxpr/ppermute | solution.py:19
  122.3 12.8 %collective-permute-start = (bf16[128,1536]{1,0:T(8,128)(2,1)}, bf16[128,1536]{1,0:T(8,128)(2,1)S(1)}, u32[]{:S(2)}, u32[]{:S(2)}) collective-permute-start(bf16[128,1536]{1,0:T(8,128)(2,1)} %get-tuple-element.1103), channel_id=1, source_target_pairs={{24,0},{0,8},{8,16},{16,24},{25,1},{1,9},{9,17},{17,25},{26,2},{2,... | collective-permute-start | bytes 1179656 | tf_op jit(solution)/shard_map/while/body/eval_jaxpr/ppermute | solution.py:19
  145.9 20.5 %collective-permute-done = bf16[128,1536]{1,0:T(8,128)(2,1)S(1)} collective-permute-done((bf16[128,1536]{1,0:T(8,128)(2,1)}, bf16[128,1536]{1,0:T(8,128)(2,1)S(1)}, u32[]{:S(2)}, u32[]{:S(2)}) %collective-permute-start) | collective-permute-done | bytes 393248 | tf_op jit(solution)/shard_map/while/body/eval_jaxpr/ppermute | solution.py:19
  166.4 14.2 %conditional.4 = (bf16[128,1536]{1,0:T(8,128)(2,1)}, bf16[2,2,128,1536]{3,2,1,0:T(8,128)(2,1)}, bf16[2,2,128,1536]{3,2,1,0:T(8,128)(2,1)}, bf16[2,2,128,64]{2,3,...) conditional(s32[]{:T(128)} %convert_element_type.166, ...), branch_computations={%region_1.1_spmd, %region_2.3_spmd} | conditional | flops 664349824 | bytes 26453752 | solution.py:213
  180.7 10.1 %collective-permute-done = bf16[128,1536]{1,0:T(8,128)(2,1)S(1)} collective-permute-done((bf16[128,1536]{1,0:T(8,128)(2,1)}, bf16[128,1536]{1,0:T(8,128)(2,1)S(1)}, u32[]{:S(2)}, u32[]{:S(2)}) %collective-permute-start) | collective-permute-done | bytes 393248 | tf_op jit(solution)/shard_map/while/body/eval_jaxpr/ppermute | solution.py:19
  190.7 14.3 %conditional.4 = (bf16[128,1536]{1,0:T(8,128)(2,1)}, bf16[2,2,128,1536]{3,2,1,0:T(8,128)(2,1)}, bf16[2,2,128,1536]{3,2,1,0:T(8,128)(2,1)}, bf16[2,2,128,64]{2,3,...) conditional(s32[]{:T(128)} %convert_element_type.166, ...), branch_computations={%region_1.1_spmd, %region_2.3_spmd} | conditional | flops 664349824 | bytes 26453752 | solution.py:213
  205.0 9.2 %collective-permute-done = bf16[128,1536]{1,0:T(8,128)(2,1)S(1)} collective-permute-done((bf16[128,1536]{1,0:T(8,128)(2,1)}, bf16[128,1536]{1,0:T(8,128)(2,1)S(1)}, u32[]{:S(2)}, u32[]{:S(2)}) %collective-permute-start) | collective-permute-done | bytes 393248 | tf_op jit(solution)/shard_map/while/body/eval_jaxpr/ppermute | solution.py:19
  215.0 12.9 %collective-permute-start = (bf16[128,1536]{1,0:T(8,128)(2,1)}, bf16[128,1536]{1,0:T(8,128)(2,1)S(1)}, u32[]{:S(2)}, u32[]{:S(2)}) collective-permute-start(bf16[128,1536]{1,0:T(8,128)(2,1)} %get-tuple-element.1103), channel_id=1, source_target_pairs={{24,0},{0,8},{8,16},{16,24},{25,1},{1,9},{9,17},{17,25},{26,2},{2,... | collective-permute-start | bytes 1179656 | tf_op jit(solution)/shard_map/while/body/eval_jaxpr/ppermute | solution.py:19
  237.7 17.1 %collective-permute-done = bf16[128,1536]{1,0:T(8,128)(2,1)S(1)} collective-permute-done((bf16[128,1536]{1,0:T(8,128)(2,1)}, bf16[128,1536]{1,0:T(8,128)(2,1)S(1)}, u32[]{:S(2)}, u32[]{:S(2)}) %collective-permute-start) | collective-permute-done | bytes 393248 | tf_op jit(solution)/shard_map/while/body/eval_jaxpr/ppermute | solution.py:19
  258.7 19.1 %collective-permute-done = bf16[128,1536]{1,0:T(8,128)(2,1)S(1)} collective-permute-done((bf16[128,1536]{1,0:T(8,128)(2,1)}, bf16[128,1536]{1,0:T(8,128)(2,1)S(1)}, u32[]{:S(2)}, u32[]{:S(2)}) %collective-permute-start) | collective-permute-done | bytes 393248 | tf_op jit(solution)/shard_map/while/body/eval_jaxpr/ppermute | solution.py:19
  281.0 193.1 %while.43 = (s32[]{:T(128)}, bf16[128,1536]{1,0:T(8,128)(2,1)S(1)}, f32[64,1536]{1,0:T(8,128)}, f32[64,1536]{1,0:T(8,128)}, s32[]{:T(128)}, /*index=5*/pred[]{:T...) while((s32[]{:T(128)}, bf16[128,1536]{1,0:T(8,128)(2,1)S(1)}, ...), condition=%wide.region_10.11_spmd, body=%wide.region_5.10_spmd.sunk | while | flops 712232064 | bytes 19004528 | solution.py:285
  281.8 16.1 %collective-permute-start.1 = (bf16[128,1536]{1,0:T(8,128)(2,1)}, bf16[128,1536]{1,0:T(8,128)(2,1)S(1)}, u32[]{:S(2)}, u32[]{:S(2)}) collective-permute-start(bf16[128,1536]{1,0:T(8,128)(2,1)} %get-tuple-element.1126), channel_id=1, source_target_pairs={{8,0},{16,8},{24,16},{0,24},{9,1},{17,9},{25,17},{1,25},{10,2},{18... | collective-permute-start | bytes 1179656 | tf_op jit(solution)/shard_map/while/body/eval_jaxpr/ppermute | solution.py:19
  304.3 16.3 %collective-permute-start.1 = (bf16[128,1536]{1,0:T(8,128)(2,1)}, bf16[128,1536]{1,0:T(8,128)(2,1)S(1)}, u32[]{:S(2)}, u32[]{:S(2)}) collective-permute-start(bf16[128,1536]{1,0:T(8,128)(2,1)} %get-tuple-element.1126), channel_id=1, source_target_pairs={{8,0},{16,8},{24,16},{0,24},{9,1},{17,9},{25,17},{1,25},{10,2},{18... | collective-permute-start | bytes 1179656 | tf_op jit(solution)/shard_map/while/body/eval_jaxpr/ppermute | solution.py:19
  320.6 9.1 %collective-permute-done.1 = bf16[128,1536]{1,0:T(8,128)(2,1)S(1)} collective-permute-done((bf16[128,1536]{1,0:T(8,128)(2,1)}, bf16[128,1536]{1,0:T(8,128)(2,1)S(1)}, u32[]{:S(2)}, u32[]{:S(2)}) %collective-permute-start.1) | collective-permute-done | bytes 393248 | tf_op jit(solution)/shard_map/while/body/eval_jaxpr/ppermute | solution.py:19
  333.8 11.7 %collective-permute-done.1 = bf16[128,1536]{1,0:T(8,128)(2,1)S(1)} collective-permute-done((bf16[128,1536]{1,0:T(8,128)(2,1)}, bf16[128,1536]{1,0:T(8,128)(2,1)S(1)}, u32[]{:S(2)}, u32[]{:S(2)}) %collective-permute-start.1) | collective-permute-done | bytes 393248 | tf_op jit(solution)/shard_map/while/body/eval_jaxpr/ppermute | solution.py:19
  345.4 13.8 %conditional.5 = (bf16[128,1536]{1,0:T(8,128)(2,1)}, f32[64,1536]{1,0:T(8,128)}, f32[64,1536]{1,0:T(8,128)}) conditional(s32[]{:T(128)} %convert_element_type.168, (f32[64,1536]{1,0:T(8,128)}, f32[64,1536]{1,0:T(8,128)}) %tuple.88, (pred[]{:T(512)}, s32[]{:T(128)}, s32[]{:T(128)}, f32[2,128,1536]{2,1,0:T(8,128)S(1)}, bf16[128,1536]{1,0:T(8,128)(2,1)S(1)}, ...), branch_computations={%region_6.6_spmd, %region_7.9_spmd} | conditional | flops 712232064 | bytes 17431224 | solution.py:276
  359.3 8.9 %collective-permute-done.1 = bf16[128,1536]{1,0:T(8,128)(2,1)S(1)} collective-permute-done((bf16[128,1536]{1,0:T(8,128)(2,1)}, bf16[128,1536]{1,0:T(8,128)(2,1)S(1)}, u32[]{:S(2)}, u32[]{:S(2)}) %collective-permute-start.1) | collective-permute-done | bytes 393248 | tf_op jit(solution)/shard_map/while/body/eval_jaxpr/ppermute | solution.py:19
  368.2 13.8 %conditional.5 = (bf16[128,1536]{1,0:T(8,128)(2,1)}, f32[64,1536]{1,0:T(8,128)}, f32[64,1536]{1,0:T(8,128)}) conditional(s32[]{:T(128)} %convert_element_type.168, (f32[64,1536]{1,0:T(8,128)}, f32[64,1536]{1,0:T(8,128)}) %tuple.88, (pred[]{:T(512)}, s32[]{:T(128)}, s32[]{:T(128)}, f32[2,128,1536]{2,1,0:T(8,128)S(1)}, bf16[128,1536]{1,0:T(8,128)(2,1)S(1)}, ...), branch_computations={%region_6.6_spmd, %region_7.9_spmd} | conditional | flops 712232064 | bytes 17431224 | solution.py:276
  382.0 8.0 %collective-permute-done.1 = bf16[128,1536]{1,0:T(8,128)(2,1)S(1)} collective-permute-done((bf16[128,1536]{1,0:T(8,128)(2,1)}, bf16[128,1536]{1,0:T(8,128)(2,1)S(1)}, u32[]{:S(2)}, u32[]{:S(2)}) %collective-permute-start.1) | collective-permute-done | bytes 393248 | tf_op jit(solution)/shard_map/while/body/eval_jaxpr/ppermute | solution.py:19
  390.8 13.9 %collective-permute-start.1 = (bf16[128,1536]{1,0:T(8,128)(2,1)}, bf16[128,1536]{1,0:T(8,128)(2,1)S(1)}, u32[]{:S(2)}, u32[]{:S(2)}) collective-permute-start(bf16[128,1536]{1,0:T(8,128)(2,1)} %get-tuple-element.1126), channel_id=1, source_target_pairs={{8,0},{16,8},{24,16},{0,24},{9,1},{17,9},{25,17},{1,25},{10,2},{18... | collective-permute-start | bytes 1179656 | tf_op jit(solution)/shard_map/while/body/eval_jaxpr/ppermute | solution.py:19
  414.4 15.2 %collective-permute-done.1 = bf16[128,1536]{1,0:T(8,128)(2,1)S(1)} collective-permute-done((bf16[128,1536]{1,0:T(8,128)(2,1)}, bf16[128,1536]{1,0:T(8,128)(2,1)S(1)}, u32[]{:S(2)}, u32[]{:S(2)}) %collective-permute-start.1) | collective-permute-done | bytes 393248 | tf_op jit(solution)/shard_map/while/body/eval_jaxpr/ppermute | solution.py:19
  429.6 13.8 %conditional.5 = (bf16[128,1536]{1,0:T(8,128)(2,1)}, f32[64,1536]{1,0:T(8,128)}, f32[64,1536]{1,0:T(8,128)}) conditional(s32[]{:T(128)} %convert_element_type.168, (f32[64,1536]{1,0:T(8,128)}, f32[64,1536]{1,0:T(8,128)}) %tuple.88, (pred[]{:T(512)}, s32[]{:T(128)}, s32[]{:T(128)}, f32[2,128,1536]{2,1,0:T(8,128)S(1)}, bf16[128,1536]{1,0:T(8,128)(2,1)S(1)}, ...), branch_computations={%region_6.6_spmd, %region_7.9_spmd} | conditional | flops 712232064 | bytes 17431224 | solution.py:276
  443.4 8.9 %collective-permute-done.1 = bf16[128,1536]{1,0:T(8,128)(2,1)S(1)} collective-permute-done((bf16[128,1536]{1,0:T(8,128)(2,1)}, bf16[128,1536]{1,0:T(8,128)(2,1)S(1)}, u32[]{:S(2)}, u32[]{:S(2)}) %collective-permute-start.1) | collective-permute-done | bytes 393248 | tf_op jit(solution)/shard_map/while/body/eval_jaxpr/ppermute | solution.py:19
  452.3 13.8 %conditional.5 = (bf16[128,1536]{1,0:T(8,128)(2,1)}, f32[64,1536]{1,0:T(8,128)}, f32[64,1536]{1,0:T(8,128)}) conditional(s32[]{:T(128)} %convert_element_type.168, (f32[64,1536]{1,0:T(8,128)}, f32[64,1536]{1,0:T(8,128)}) %tuple.88, (pred[]{:T(512)}, s32[]{:T(128)}, s32[]{:T(128)}, f32[2,128,1536]{2,1,0:T(8,128)S(1)}, bf16[128,1536]{1,0:T(8,128)(2,1)S(1)}, ...), branch_computations={%region_6.6_spmd, %region_7.9_spmd} | conditional | flops 712232064 | bytes 17431224 | solution.py:276
  466.1 8.0 %collective-permute-done.1 = bf16[128,1536]{1,0:T(8,128)(2,1)S(1)} collective-permute-done((bf16[128,1536]{1,0:T(8,128)(2,1)}, bf16[128,1536]{1,0:T(8,128)(2,1)S(1)}, u32[]{:S(2)}, u32[]{:S(2)}) %collective-permute-start.1) | collective-permute-done | bytes 393248 | tf_op jit(solution)/shard_map/while/body/eval_jaxpr/ppermute | solution.py:19
  478.5 27.4 %reduce-scatter.7.cloned.1.call-done = f32[192,64]{1,0:T(8,128)} async-done(((f32[1536,64]{1,0:T(8,128)}), f32[192,64]{1,0:T(8,128)}) %reduce-scatter.7.cloned.1.call-update) | async-done | bytes 49168
  507.5 30.8 %reduce-scatter.9.cloned.1.call-done = f32[192,64]{1,0:T(8,128)} async-done(((f32[1536,64]{1,0:T(8,128)}), f32[192,64]{1,0:T(8,128)}) %reduce-scatter.9.cloned.1.call-update) | async-done | bytes 49168
  (189 shorter events, 188.9 us)
Async XLA Ops:
  7.2 1.5 copy-start
  7.2 56.4 %all-gather.3.cloned.1.call-start = ((), (), s32[]{:S(2)}) async-start(), calls=%async_computation.2 | async-start | bytes 5308416 | tf_op jit(solution)/shard_map/all_gather | solution.py:123
  7.9 498.0 %reduce-scatter.7.cloned.1.call-start = ((), (), s32[]{:S(2)}) async-start(), calls=%async_computation.3 | async-start | bytes 884736
  79.9 1.4 copy-start.1
  83.4 12.4 %collective-permute-start = (bf16[128,1536]{1,0:T(8,128)(2,1)}, bf16[128,1536]{1,0:T(8,128)(2,1)S(1)}, u32[]{:S(2)}, u32[]{:S(2)}) collective-permute-start(bf16[128,1536]{1,0:T(8,128)(2,1)} %get-tuple-element.1103), channel_id=1, source_target_pairs={{24,0},{0,8},{8,16},{16,24},{25,1},{1,9},{9,17},{17,25},{26,2},{2,... | collective-permute-start | bytes 1179656 | tf_op jit(solution)/shard_map/while/body/eval_jaxpr/ppermute | solution.py:19
  103.1 1.0 copy-start.3
  106.5 1.4 copy-start.1
  110.0 11.5 %collective-permute-start = (bf16[128,1536]{1,0:T(8,128)(2,1)}, bf16[128,1536]{1,0:T(8,128)(2,1)S(1)}, u32[]{:S(2)}, u32[]{:S(2)}) collective-permute-start(bf16[128,1536]{1,0:T(8,128)(2,1)} %get-tuple-element.1103), channel_id=1, source_target_pairs={{24,0},{0,8},{8,16},{16,24},{25,1},{1,9},{9,17},{17,25},{26,2},{2,... | collective-permute-start | bytes 1179656 | tf_op jit(solution)/shard_map/while/body/eval_jaxpr/ppermute | solution.py:19
  122.3 20.5 %collective-permute-start = (bf16[128,1536]{1,0:T(8,128)(2,1)}, bf16[128,1536]{1,0:T(8,128)(2,1)S(1)}, u32[]{:S(2)}, u32[]{:S(2)}) collective-permute-start(bf16[128,1536]{1,0:T(8,128)(2,1)} %get-tuple-element.1103), channel_id=1, source_target_pairs={{24,0},{0,8},{8,16},{16,24},{25,1},{1,9},{9,17},{17,25},{26,2},{2,... | collective-permute-start | bytes 1179656 | tf_op jit(solution)/shard_map/while/body/eval_jaxpr/ppermute | solution.py:19
  143.5 22.9 %collective-permute-start = (bf16[128,1536]{1,0:T(8,128)(2,1)}, bf16[128,1536]{1,0:T(8,128)(2,1)S(1)}, u32[]{:S(2)}, u32[]{:S(2)}) collective-permute-start(bf16[128,1536]{1,0:T(8,128)(2,1)} %get-tuple-element.1103), channel_id=1, source_target_pairs={{24,0},{0,8},{8,16},{16,24},{25,1},{1,9},{9,17},{17,25},{26,2},{2,... | collective-permute-start | bytes 1179656 | tf_op jit(solution)/shard_map/while/body/eval_jaxpr/ppermute | solution.py:19
  173.8 1.0 copy-start.3
  177.2 1.4 copy-start.1
  180.7 10.1 %collective-permute-start = (bf16[128,1536]{1,0:T(8,128)(2,1)}, bf16[128,1536]{1,0:T(8,128)(2,1)S(1)}, u32[]{:S(2)}, u32[]{:S(2)}) collective-permute-start(bf16[128,1536]{1,0:T(8,128)(2,1)} %get-tuple-element.1103), channel_id=1, source_target_pairs={{24,0},{0,8},{8,16},{16,24},{25,1},{1,9},{9,17},{17,25},{26,2},{2,... | collective-permute-start | bytes 1179656 | tf_op jit(solution)/shard_map/while/body/eval_jaxpr/ppermute | solution.py:19
  201.5 1.4 copy-start.1
  205.0 9.2 %collective-permute-start = (bf16[128,1536]{1,0:T(8,128)(2,1)}, bf16[128,1536]{1,0:T(8,128)(2,1)S(1)}, u32[]{:S(2)}, u32[]{:S(2)}) collective-permute-start(bf16[128,1536]{1,0:T(8,128)(2,1)} %get-tuple-element.1103), channel_id=1, source_target_pairs={{24,0},{0,8},{8,16},{16,24},{25,1},{1,9},{9,17},{17,25},{26,2},{2,... | collective-permute-start | bytes 1179656 | tf_op jit(solution)/shard_map/while/body/eval_jaxpr/ppermute | solution.py:19
  215.0 19.5 %collective-permute-start = (bf16[128,1536]{1,0:T(8,128)(2,1)}, bf16[128,1536]{1,0:T(8,128)(2,1)S(1)}, u32[]{:S(2)}, u32[]{:S(2)}) collective-permute-start(bf16[128,1536]{1,0:T(8,128)(2,1)} %get-tuple-element.1103), channel_id=1, source_target_pairs={{24,0},{0,8},{8,16},{16,24},{25,1},{1,9},{9,17},{17,25},{26,2},{2,... | collective-permute-start | bytes 1179656 | tf_op jit(solution)/shard_map/while/body/eval_jaxpr/ppermute | solution.py:19
  235.3 19.5 %collective-permute-start = (bf16[128,1536]{1,0:T(8,128)(2,1)}, bf16[128,1536]{1,0:T(8,128)(2,1)S(1)}, u32[]{:S(2)}, u32[]{:S(2)}) collective-permute-start(bf16[128,1536]{1,0:T(8,128)(2,1)} %get-tuple-element.1103), channel_id=1, source_target_pairs={{24,0},{0,8},{8,16},{16,24},{25,1},{1,9},{9,17},{17,25},{26,2},{2,... | collective-permute-start | bytes 1179656 | tf_op jit(solution)/shard_map/while/body/eval_jaxpr/ppermute | solution.py:19
  255.6 22.1 %collective-permute-start = (bf16[128,1536]{1,0:T(8,128)(2,1)}, bf16[128,1536]{1,0:T(8,128)(2,1)S(1)}, u32[]{:S(2)}, u32[]{:S(2)}) collective-permute-start(bf16[128,1536]{1,0:T(8,128)(2,1)} %get-tuple-element.1103), channel_id=1, source_target_pairs={{24,0},{0,8},{8,16},{16,24},{25,1},{1,9},{9,17},{17,25},{26,2},{2,... | collective-permute-start | bytes 1179656 | tf_op jit(solution)/shard_map/while/body/eval_jaxpr/ppermute | solution.py:19
  281.8 21.7 %collective-permute-start.1 = (bf16[128,1536]{1,0:T(8,128)(2,1)}, bf16[128,1536]{1,0:T(8,128)(2,1)S(1)}, u32[]{:S(2)}, u32[]{:S(2)}) collective-permute-start(bf16[128,1536]{1,0:T(8,128)(2,1)} %get-tuple-element.1126), channel_id=1, source_target_pairs={{8,0},{16,8},{24,16},{0,24},{9,1},{17,9},{25,17},{1,25},{10,2},{18... | collective-permute-start | bytes 1179656 | tf_op jit(solution)/shard_map/while/body/eval_jaxpr/ppermute | solution.py:19
  304.3 25.4 %collective-permute-start.1 = (bf16[128,1536]{1,0:T(8,128)(2,1)}, bf16[128,1536]{1,0:T(8,128)(2,1)S(1)}, u32[]{:S(2)}, u32[]{:S(2)}) collective-permute-start(bf16[128,1536]{1,0:T(8,128)(2,1)} %get-tuple-element.1126), channel_id=1, source_target_pairs={{8,0},{16,8},{24,16},{0,24},{9,1},{17,9},{25,17},{1,25},{10,2},{18... | collective-permute-start | bytes 1179656 | tf_op jit(solution)/shard_map/while/body/eval_jaxpr/ppermute | solution.py:19
  330.5 15.0 %collective-permute-start.1 = (bf16[128,1536]{1,0:T(8,128)(2,1)}, bf16[128,1536]{1,0:T(8,128)(2,1)S(1)}, u32[]{:S(2)}, u32[]{:S(2)}) collective-permute-start(bf16[128,1536]{1,0:T(8,128)(2,1)} %get-tuple-element.1126), channel_id=1, source_target_pairs={{8,0},{16,8},{24,16},{0,24},{9,1},{17,9},{25,17},{1,25},{10,2},{18... | collective-permute-start | bytes 1179656 | tf_op jit(solution)/shard_map/while/body/eval_jaxpr/ppermute | solution.py:19
  345.4 1.8 copy-start.4
  359.3 8.9 %collective-permute-start.1 = (bf16[128,1536]{1,0:T(8,128)(2,1)}, bf16[128,1536]{1,0:T(8,128)(2,1)S(1)}, u32[]{:S(2)}, u32[]{:S(2)}) collective-permute-start(bf16[128,1536]{1,0:T(8,128)(2,1)} %get-tuple-element.1126), channel_id=1, source_target_pairs={{8,0},{16,8},{24,16},{0,24},{9,1},{17,9},{25,17},{1,25},{10,2},{18... | collective-permute-start | bytes 1179656 | tf_op jit(solution)/shard_map/while/body/eval_jaxpr/ppermute | solution.py:19
  368.2 1.8 copy-start.4
  382.0 8.0 %collective-permute-start.1 = (bf16[128,1536]{1,0:T(8,128)(2,1)}, bf16[128,1536]{1,0:T(8,128)(2,1)S(1)}, u32[]{:S(2)}, u32[]{:S(2)}) collective-permute-start(bf16[128,1536]{1,0:T(8,128)(2,1)} %get-tuple-element.1126), channel_id=1, source_target_pairs={{8,0},{16,8},{24,16},{0,24},{9,1},{17,9},{25,17},{1,25},{10,2},{18... | collective-permute-start | bytes 1179656 | tf_op jit(solution)/shard_map/while/body/eval_jaxpr/ppermute | solution.py:19
  390.8 19.5 %collective-permute-start.1 = (bf16[128,1536]{1,0:T(8,128)(2,1)}, bf16[128,1536]{1,0:T(8,128)(2,1)S(1)}, u32[]{:S(2)}, u32[]{:S(2)}) collective-permute-start(bf16[128,1536]{1,0:T(8,128)(2,1)} %get-tuple-element.1126), channel_id=1, source_target_pairs={{8,0},{16,8},{24,16},{0,24},{9,1},{17,9},{25,17},{1,25},{10,2},{18... | collective-permute-start | bytes 1179656 | tf_op jit(solution)/shard_map/while/body/eval_jaxpr/ppermute | solution.py:19
  411.1 18.5 %collective-permute-start.1 = (bf16[128,1536]{1,0:T(8,128)(2,1)}, bf16[128,1536]{1,0:T(8,128)(2,1)S(1)}, u32[]{:S(2)}, u32[]{:S(2)}) collective-permute-start(bf16[128,1536]{1,0:T(8,128)(2,1)} %get-tuple-element.1126), channel_id=1, source_target_pairs={{8,0},{16,8},{24,16},{0,24},{9,1},{17,9},{25,17},{1,25},{10,2},{18... | collective-permute-start | bytes 1179656 | tf_op jit(solution)/shard_map/while/body/eval_jaxpr/ppermute | solution.py:19
  429.6 1.8 copy-start.4
  443.4 8.9 %collective-permute-start.1 = (bf16[128,1536]{1,0:T(8,128)(2,1)}, bf16[128,1536]{1,0:T(8,128)(2,1)S(1)}, u32[]{:S(2)}, u32[]{:S(2)}) collective-permute-start(bf16[128,1536]{1,0:T(8,128)(2,1)} %get-tuple-element.1126), channel_id=1, source_target_pairs={{8,0},{16,8},{24,16},{0,24},{9,1},{17,9},{25,17},{1,25},{10,2},{18... | collective-permute-start | bytes 1179656 | tf_op jit(solution)/shard_map/while/body/eval_jaxpr/ppermute | solution.py:19
  452.3 1.8 copy-start.4
  466.1 8.0 %collective-permute-start.1 = (bf16[128,1536]{1,0:T(8,128)(2,1)}, bf16[128,1536]{1,0:T(8,128)(2,1)S(1)}, u32[]{:S(2)}, u32[]{:S(2)}) collective-permute-start(bf16[128,1536]{1,0:T(8,128)(2,1)} %get-tuple-element.1126), channel_id=1, source_target_pairs={{8,0},{16,8},{24,16},{0,24},{9,1},{17,9},{25,17},{1,25},{10,2},{18... | collective-permute-start | bytes 1179656 | tf_op jit(solution)/shard_map/while/body/eval_jaxpr/ppermute | solution.py:19
  476.3 62.0 %reduce-scatter.9.cloned.1.call-start = ((), (), s32[]{:S(2)}) async-start(), calls=%async_computation.4 | async-start | bytes 884736
  (3 other events, 2.9 us)
Sparse Core Ops, SparseCore 0:
  9.6 53.9 all-gather.2
  476.4 29.4 reduce-scatter.6
  508.2 30.0 reduce-scatter.8
where the time goes:
time: 548 us; the launch traced here: 546 us
  waiting for transfers between devices  306 us (56%)
  starting transfers between devices  86.5 us (16%)
  matrix products  71.6 us (13%)
  other arithmetic  34.5 us (6%)
  local copies, waits for them, and re-layouts  34.1 us (6%)
  between operations  13.8 us (3%)
    ppermute x18, waiting for transfers between devices, from_behind(): return lax.ppermute(block, axis, route)  195 us
    ppermute x18, starting transfers between devices, from_behind(): return lax.ppermute(block, axis, route)  86.4 us
    unnamed x5, waiting for transfers between devices  58.9 us
    all_gather x1, waiting for transfers between devices, local(): layer_weight = lax.all_gather(frozen_weight[0], 'dp', axis=0, tiled=True)  51.6 us
    dot_general x4, matrix products, forward_layer_pass(): jnp.dot(normalized_hidden, layer_weight, preferred_element_type=jnp.float32)  16.2 us
    dot_general x4, matrix products, backward_layer_pass(): lax.dot_general(preactivation_gradient, layer_weight, (((1,), (1,)), ((),...  15.8 us
    dynamic_update_slice x8, other arithmetic, place_block(): return lax.dynamic_update_slice(store, value[None, None], starts)  12.4 us
    another operation x16, local copies, waits for them, and re-layouts  12.2 us
  transfers between devices with their start and end apart: 21, of which 21 were waited for; matrix products, arithmetic and copies ran while one was open for 1% of the time, Pallas kernels for 0%

commit v1 on v0

v1 whole, which is shorter than its diff:
```python
import math

import jax
import jax.numpy as jnp
from jax import lax
from jax.sharding import PartitionSpec as P

BLEND = 0.5
ADAPTER_SCALE = 0.5
EPSILON = 1e-06


def forward_layer_pass(
    hidden_state, layer_weight, down_weight_rows, up_weight_rows, gain_row, modulate_row
):
    hidden_float = hidden_state.astype(jnp.float32)
    inverse_rms = lax.rsqrt(jnp.mean(hidden_float * hidden_float, axis=-1, keepdims=True) + EPSILON)
    normalized_hidden = (hidden_float * inverse_rms * (gain_row * modulate_row)).astype(
        jnp.bfloat16
    )
    low_rank_hidden = lax.dot_general(
        normalized_hidden,
        down_weight_rows,
        (((1,), (1,)), ((), ())),
        preferred_element_type=jnp.float32,
    ).astype(jnp.bfloat16)
    preactivation = jnp.dot(
        normalized_hidden, layer_weight, preferred_element_type=jnp.float32
    ) + ADAPTER_SCALE * jnp.dot(low_rank_hidden, up_weight_rows, preferred_element_type=jnp.float32)
    output = (hidden_float + jax.nn.silu(preactivation)).astype(jnp.bfloat16)
    return (output, normalized_hidden, low_rank_hidden, preactivation)


def backward_layer_pass(
    hidden_state,
    normalized_hidden,
    low_rank_hidden,
    preactivation,
    output_gradient,
    layer_weight,
    down_weight_rows,
    up_weight_rows,
    gain_row,
    modulate_row,
):
    sigmoid_value = jax.nn.sigmoid(preactivation)
    preactivation_gradient = (
        output_gradient * sigmoid_value * (1.0 + preactivation * (1.0 - sigmoid_value))
    ).astype(jnp.bfloat16)
    low_rank_gradient = (
        ADAPTER_SCALE
        * lax.dot_general(
            preactivation_gradient,
            up_weight_rows,
            (((1,), (1,)), ((), ())),
            preferred_element_type=jnp.float32,
        )
    ).astype(jnp.bfloat16)
    norm_grad = lax.dot_general(
        preactivation_gradient,
        layer_weight,
        (((1,), (1,)), ((), ())),
        preferred_element_type=jnp.float32,
    ) + jnp.dot(low_rank_gradient, down_weight_rows, preferred_element_type=jnp.float32)
    up_gradient_term = ADAPTER_SCALE * lax.dot_general(
        low_rank_hidden,
        preactivation_gradient,
        (((0,), (0,)), ((), ())),
        preferred_element_type=jnp.float32,
    )
    down_gradient_term = lax.dot_general(
        low_rank_gradient,
        normalized_hidden,
        (((0,), (0,)), ((), ())),
        preferred_element_type=jnp.float32,
    )
    hidden_float = hidden_state.astype(jnp.float32)
    inverse_rms = lax.rsqrt(jnp.mean(hidden_float * hidden_float, axis=-1, keepdims=True) + EPSILON)
    scaled = hidden_float * inverse_rms
    scaled_grad = norm_grad * (gain_row * modulate_row)
    hidden_gradient = output_gradient + inverse_rms * (
        scaled_grad - scaled * jnp.mean(scaled_grad * scaled, axis=-1, keepdims=True)
    )
    return (hidden_gradient, down_gradient_term, up_gradient_term)


def local(
    latent,
    target,
    camera_of_token,
    timestep_indices,
    camera_embedding_table,
    timestep_embedding_table,
    layer_norm_gain,
    frozen_weight,
    adapter_down_weight,
    adapter_up_weight,
):
    sections = lax.axis_size("section")
    ways = lax.axis_size("dp")
    position = lax.axis_index("section")
    width = latent.shape[1]
    rank = adapter_down_weight.shape[1]
    rows = latent.shape[0] // sections
    scale_factor = 1.0 / math.sqrt(latent.shape[0] * ways)
    weights = lax.all_gather(
        frozen_weight[0], ("section", "dp"), axis=0, tiled=True
    ).reshape(sections, width, width)
    adapters = lax.all_gather(
        jnp.concatenate([adapter_down_weight, adapter_up_weight], axis=1), "section", axis=0, tiled=True
    )
    down, up = adapters[:, :rank], adapters[:, rank:]
    gains = lax.all_gather(layer_norm_gain, "section", axis=0, tiled=True)
    mine = lambda array: lax.dynamic_slice_in_dim(array, position * rows, rows, 0)
    latent, target, camera_of_token = mine(latent), mine(target), mine(camera_of_token)
    camera_rows = jnp.dot(
        jax.nn.one_hot(camera_of_token, camera_embedding_table.shape[0], dtype=jnp.bfloat16),
        camera_embedding_table,
        preferred_element_type=jnp.float32,
    )
    modulation = 1.0 + jnp.dot(
        jax.nn.one_hot(timestep_indices, timestep_embedding_table.shape[0], dtype=jnp.bfloat16),
        timestep_embedding_table,
        preferred_element_type=jnp.float32,
    )
    saved = {}
    current = latent
    for step in range(2):
        hidden = (current.astype(jnp.float32) + camera_rows).astype(jnp.bfloat16)
        for layer in range(sections):
            output, *rest = forward_layer_pass(
                hidden, weights[layer], down[layer], up[layer], gains[layer], modulation[step]
            )
            saved[step, layer] = (hidden, *rest)
            hidden = output
        final = BLEND * (current.astype(jnp.float32) + hidden.astype(jnp.float32))
        current = final.astype(jnp.bfloat16)
    squashed = jnp.tanh(final)
    adjoint = target.astype(jnp.float32) * (1.0 - squashed * squashed) * scale_factor
    down_sum, up_sum = [0.0] * sections, [0.0] * sections
    cotangent = BLEND * adjoint
    for step in (1, 0):
        for layer in reversed(range(sections)):
            gradient, down_term, up_term = backward_layer_pass(
                *saved[step, layer],
                cotangent,
                weights[layer],
                down[layer],
                up[layer],
                gains[layer],
                modulation[step],
            )
            down_sum[layer] = down_sum[layer] + down_term
            up_sum[layer] = up_sum[layer] + up_term
            cotangent = gradient.astype(jnp.bfloat16).astype(jnp.float32)
        cotangent = BLEND * (BLEND * adjoint + cotangent)
    sums = jnp.concatenate([jnp.stack(down_sum), jnp.stack(up_sum)], axis=1)
    sums = sums.reshape(sections, 2 * rank, ways, width // ways).transpose(0, 2, 1, 3)
    sums = sums.reshape(sections * ways, 2 * rank, width // ways)
    part = lax.psum_scatter(sums, ("section", "dp"), scatter_dimension=0, tiled=True)
    return (part[:, :rank], part[:, rank:])


def solution(mesh):
    in_specs = (
        P("dp", None),
        P("dp", None),
        P("dp"),
        P(),
        P(),
        P(),
        P("section", None),
        P("section", "dp", None),
        P("section", None, None),
        P("section", None, None),
    )
    out_specs = (P("section", None, "dp"), P("section", None, "dp"))
    return jax.shard_map(local, mesh=mesh, in_specs=in_specs, out_specs=out_specs, check_vma=False)
```

time: 548 us -> 375 us (0.68)
  starting transfers between devices: 86.5 us -> 0.12 us
  other arithmetic: 34.5 us -> 5.8 us
  local copies, waits for them, and re-layouts: 34.1 us -> 7.99 us
  matrix products: 71.6 us -> 46.6 us
  waiting for transfers between devices: 306 us -> 290 us
  blocking collectives: 0 us -> 9.8 us
    ppermute x18 -> x0, waiting for transfers between devices: 195 us -> none  [from_behind(): return lax.ppermute(block, axis, route)]
    reduce_scatter x0 -> x1, waiting for transfers between devices: none -> 142 us  [local(): lax.psum_scatter(sums, ('section', 'dp'), scatter_dimension=0, tiled=True)]
    all_gather x1 -> x2, waiting for transfers between devices: 51.6 us -> 146 us  [the longest x1 126 us: local(): lax.all_gather(frozen_weight[0], ('section', 'dp'), axis=0, tiled=True)]
    ppermute x18 -> x0, starting transfers between devices: 86.4 us -> none  [from_behind(): return lax.ppermute(block, axis, route)]
    unnamed x5 -> x3, waiting for transfers between devices: 58.9 us -> 0.73 us
    dynamic_update_slice x12 -> x0, other arithmetic: 12.8 us -> none  [the longest x8 12.4 us: place_block(): return lax.dynamic_update_slice(store, value[None, None], starts)]
    another operation x16 -> x0, local copies, waits for them, and re-layouts: 12.2 us -> none
    all_gather x0 -> x1, blocking collectives: none -> 9.8 us  [local(): gains = lax.all_gather(layer_norm_gain, 'section', axis=0, tiled=True)]
  transfers between devices with their start and end apart: 21 -> 3, of which waited for: 21 -> 3; matrix products, arithmetic and copies ran while one was open for 1% -> 1% of each run, Pallas kernels for 0% -> 0%
where the time goes in v1:
time: 375 us; the launch traced here: 374 us
  waiting for transfers between devices  290 us (77%)
  matrix products  46.6 us (12%)
  between operations  14.3 us (4%)
  blocking collectives  9.8 us (3%)
  local copies, waits for them, and re-layouts  7.99 us (2%)
  other arithmetic  5.8 us (2%)
    reduce_scatter x1, waiting for transfers between devices, local(): lax.psum_scatter(sums, ('section', 'dp'), scatter_dimension=0, tiled=True)  142 us
    all_gather x1, waiting for transfers between devices, local(): lax.all_gather(frozen_weight[0], ('section', 'dp'), axis=0, tiled=True)  126 us
    all_gather x1, waiting for transfers between devices, local(): lax.all_gather(jnp.concatenate([adapter_down_weight, adapter_up_weight],...  20.7 us
    dot_general x8, matrix products, forward_layer_pass(): jnp.dot(normalized_hidden, layer_weight, preferred_element_type=jnp.float32)  15.9 us
    dot_general x7, matrix products, backward_layer_pass(): lax.dot_general(preactivation_gradient, layer_weight, (((1,), (1,)), ((),...  10.7 us
    all_gather x1, blocking collectives, local(): gains = lax.all_gather(layer_norm_gain, 'section', axis=0, tiled=True)  9.8 us
  transfers between devices with their start and end apart: 3, of which 3 were waited for; matrix products, arithmetic and copies ran while one was open for 1% of the time, Pallas kernels for 0%

profile of v1, /device:TPU:0, one launch (start us, length us, event | category | flops | bytes accessed | tf_op | source)
XLA Modules:
  0.0 374.2 jit_solution(13954476180291516710)
XLA Ops:
  7.2 1.8 pad_maximum_fusion
  9.9 0.8 dynamic_slice.11
  10.6 9.8 %all-gather.1 = f32[4,1,1536]{2,1,0:T(1,128)S(1)} all-gather(f32[1,1,1536]{2,1,0:T(1,128)} %bitcast.203), channel_id=1, replica_groups=mesh['section'=4,'dp'=8] {'section'}, dimensions={0}, use_global_device_ids=true | all-gather | bytes 30720 | tf_op jit(solution)/shard_map/all_gather | solution.py:113
  20.4 0.9 convolution_add_fusion.15
  21.4 1.3 fusion.128
  22.8 20.7 %all-gather.5.cloned.1.call-done = bf16[4,128,1536]{2,1,0:T(8,128)(2,1)} async-done(((bf16[1,128,1536]{2,1,0:T(8,128)(2,1)}), bf16[4,128,1536]{2,1,0:T(8,128)(2,1)}) %all-gather.5.cloned.1.call-update) | async-done | bytes 1572880 | tf_op jit(solution)/shard_map/all_gather | solution.py:109
  43.4 1.3 convolution_convert_fusion.7
  44.7 125.8 %all-gather.7.cloned.1.call-done = bf16[1,6144,1536]{2,1,0:T(8,128)(2,1)} async-done(((bf16[1,192,1536]{2,1,0:T(8,128)(2,1)}), bf16[1,6144,1536]{2,1,0:T(8,128)(2,1)}) %all-gather.7.cloned.1.call-update) | async-done | bytes 18874384 | tf_op jit(solution)/shard_map/all_gather | solution.py:106
  170.5 3.3 fusion.2
  174.5 3.6 fusion.6
  178.8 4.1 %fusion.10 = f32[64,1536]{1,0:T(8,128)S(1)} fusion(bf16[1,6144,1536]{2,1,0:T(8,128)(2,1)} %all-gather.7.cloned.1.call-done, bf16[64,1536]{1,0:T(8,128)(2,1)S(1)} %get-tuple-element.36, f32[1536]{0:T(1024)S(1)} %get-tuple-element.6, f32[64]{0:T(128)S(1)} %add_rsqrt_fusion.5), kind=kOutput, calls=%fused_computation.15 | convolution fusion | flops 302383104 | bytes 5314816 | tf_op jit(solution)/shard_map/dot_general | solution.py:27
  183.6 1.0 fusion.14
  184.6 1.4 fusion.138
  186.3 1.0 fusion.1
  187.9 1.0 fusion.5
  189.6 1.0 fusion.9
  191.0 1.0 fusion.13
  192.2 1.4 multiply_convert_fusion.2
  194.3 1.5 fusion.12
  197.2 1.5 fusion.8
  200.0 1.5 fusion.4
  202.5 1.0 fusion.165
  203.5 1.5 fusion
  205.9 1.5 fusion.11
  208.2 1.5 fusion.7
  210.5 1.5 fusion.3
  214.4 1.7 fusion.34
  216.1 1.8 maximum_maximum_fusion
  218.0 2.4 copy.15
  220.3 3.3 copy.16
  223.7 142.4 %reduce-scatter.2.cloned.1.call-done = f32[1,128,192]{2,1,0:T(8,128)} async-done(((f32[32,128,192]{2,1,0:T(8,128)}), f32[1,128,192]{2,1,0:T(8,128)}) %reduce-scatter.2.cloned.1.call-update) | async-done | bytes 98320 | tf_op jit(solution)/shard_map/reduce_scatter | solution.py:160
  366.1 1.5 fusion.197
  (78 shorter events, 14.1 us)
Async XLA Ops:
  7.2 13.3 %copy-start = (bf16[50,1536]{1,0:T(8,128)(2,1)S(1)}, bf16[50,1536]{1,0:T(8,128)(2,1)}, u32[]{:S(2)}) copy-start(bf16[50,1536]{1,0:T(8,128)(2,1)} %param.15) | copy-start | bytes 460804
  7.2 36.2 %all-gather.5.cloned.1.call-start = ((), (), s32[]{:S(2)}) async-start(), calls=%async_computation.1 | async-start | bytes 1966080 | tf_op jit(solution)/shard_map/all_gather | solution.py:109
  9.1 161.4 %all-gather.7.cloned.1.call-start = ((), (), s32[]{:S(2)}) async-start(), calls=%async_computation.3 | async-start | bytes 19464192 | tf_op jit(solution)/shard_map/all_gather | solution.py:106
  9.8 356.3 %reduce-scatter.2.cloned.1.call-start = ((), (), s32[]{:S(2)}) async-start(), calls=%async_computation.2 | async-start | bytes 4325376 | tf_op jit(solution)/shard_map/reduce_scatter | solution.py:160
  22.7 160.1 %copy-start.2 = (bf16[64,1536]{1,0:T(8,128)(2,1)}, bf16[64,1536]{1,0:T(8,128)(2,1)S(1)}, u32[]{:S(2)}) copy-start(bf16[64,1536]{1,0:T(8,128)(2,1)S(1)} %get-tuple-element.40) | copy-start | bytes 589828
  43.4 130.4 %copy-start.1 = (bf16[4,128,1536]{2,1,0:T(8,128)(2,1)S(1)}, bf16[4,128,1536]{2,1,0:T(8,128)(2,1)}, u32[]{:S(2)}) copy-start(bf16[4,128,1536]{2,1,0:T(8,128)(2,1)} %all-gather.5.cloned.1.call-done) | copy-start | bytes 4718596
  173.8 9.7 %copy-start.3 = (bf16[1,6144,1536]{2,1,0:T(8,128)(2,1)S(1)}, bf16[1,6144,1536]{2,1,0:T(8,128)(2,1)}, u32[]{:S(2)}) copy-start(bf16[1,6144,1536]{2,1,0:T(8,128)(2,1)} %all-gather.7.cloned.1.call-done) | copy-start | bytes 56623108
Sparse Core Ops, SparseCore 0:
  9.8 33.5 all-gather.4
  46.5 124.0 all-gather.6
  223.8 142.2 reduce-scatter.1

commit v2 on v1

v2 whole, which is shorter than its diff:
```python
import functools
import math

import jax
import jax.numpy as jnp
from jax import lax
from jax.experimental import pallas as pl
from jax.experimental.pallas import tpu as pltpu
from jax.sharding import PartitionSpec as P

BLEND = 0.5
ADAPTER_SCALE = 0.5
EPSILON = 1e-06
MESH = pl.DeviceIdType.MESH
NT = (((1,), (1,)), ((), ()))
TN = (((0,), (0,)), ((), ()))


def bits_of(size):
    bits = size.bit_length() - 1
    return bits if 2**bits == size else 0


def section_at(place, size):
    bits = bits_of(size)
    if not bits:
        return place
    bit = [(place // 2**i) % 2 for i in range(bits)] + [0]
    return sum(((bit[i] + bit[i + 1]) % 2) * 2**i for i in range(bits))


def place_of(section, size):
    bits = bits_of(size)
    if not bits:
        return section
    upper, place = 0, 0
    for i in reversed(range(bits)):
        upper = ((section // 2**i) % 2 + upper) % 2
        place = place + upper * 2**i
    return place


def arrivals(size):
    half = size // 2
    steps = []
    for distance in range(1, half + 1):
        for way in (1, -1):
            if distance < half or size % 2:
                steps.append((way, distance, None))
            else:
                steps.append((way, distance, 0 if way == 1 else 1))
    return steps


def part_at(distance, way, size):
    if distance < size // 2 or size % 2:
        return None
    return 0 if way == 1 else 1


def kernel(
    sections,
    ways,
    scale_factor,
    steps_ref,
    latent_ref,
    target_ref,
    camera_ref,
    camera_table_ref,
    step_table_ref,
    gain_ref,
    shard_ref,
    down_ref,
    up_ref,
    out_ref,
    weights,
    adapters,
    gains,
    hidden_at,
    pre_at,
    low_at,
    modulation,
    camera_rows,
    adjoint_at,
    pair_out,
    pair_in,
    depth_out,
    depth_in,
    plane_out,
    plane_in,
    local_sem,
    first_send,
    first_recv,
    second_send,
    second_recv,
    twin_send,
    twin_recv,
    small_send,
    small_recv,
    adapter_send,
    adapter_recv,
    pair_sems,
    depth_send,
    depth_recv,
    plane_send,
    plane_recv,
):
    section, lane = lax.axis_index("section"), lax.axis_index("dp")
    depth_size = ways // 2
    depth, core = lane // 2, lane % 2
    place = place_of(section, sections)
    block, width = shard_ref.shape
    rows = hidden_at.shape[2]
    rank = down_ref.shape[0]
    twin = (section, depth * 2 + 1 - core)

    def on_section(other):
        return (other, lane)

    def on_depth(other):
        return (section, other * 2 + core)

    barrier = pltpu.get_barrier_semaphore()
    friends = [twin]
    friends += [on_section((section + k) % sections) for k in range(1, sections)]
    friends += [on_depth((depth + k) % depth_size) for k in range(1, depth_size)]
    for friend in friends:
        pl.semaphore_signal(barrier, inc=1, device_id=friend, device_id_type=MESH)
    pl.semaphore_wait(barrier, len(friends))

    def remote(source, target, send, recv, device):
        return pltpu.make_async_remote_copy(
            src_ref=source,
            dst_ref=target,
            send_sem=send,
            recv_sem=recv,
            device_id=device,
            device_id_type=MESH,
        )

    pending = []

    def go(copy):
        copy.start()
        pending.append(copy)

    go_gain, go_adapter = [], []
    for k in range(1, sections):
        other = on_section((section + k) % sections)
        copy = remote(gain_ref, gains.at[section], small_send.at[k], small_recv.at[k], other)
        copy.start()
        go_gain.append((copy, k))

    def region(home, row, half, part):
        columns = width // 2
        start = half * columns
        if part is not None:
            columns = columns // 2
            start = start + part * columns
        offset = pl.multiple_of((row * 2 + core) * block, block)
        return weights.at[home, pl.ds(offset, block), pl.ds(start, columns)]

    def own(half, part):
        columns = width // 2
        start = half * columns
        if part is not None:
            columns = columns // 2
            start = start + part * columns
        return shard_ref.at[:, pl.ds(start, columns)]

    local = [
        pltpu.make_async_copy(
            shard_ref,
            weights.at[section, pl.ds(pl.multiple_of(lane * block, block), block), :],
            local_sem.at[0],
        ),
        pltpu.make_async_copy(gain_ref, gains.at[section], local_sem.at[1]),
        pltpu.make_async_copy(down_ref, adapters.at[section, 0], local_sem.at[2]),
        pltpu.make_async_copy(up_ref, adapters.at[section, 1], local_sem.at[3]),
    ]
    for copy in local:
        copy.start()

    sizes = ((sections, depth_size), (depth_size, sections))
    spots = ((place, depth), (depth, place))

    def item(half, first, second):
        at_first = (spots[half][0] - first) % sizes[half][0]
        at_second = (spots[half][1] - second) % sizes[half][1]
        if half == 0:
            return section_at(at_first, sections), at_second
        return section_at(at_second, sections), at_first

    def neighbour(half, ring, way):
        if (half + ring) % 2 == 0:
            return on_section(section_at((place + way) % sections, sections))
        return on_depth((depth + way) % depth_size)

    def send(half, ring, first, second, way, distance):
        part = part_at(distance, way, sizes[half][ring])
        home, row = item(half, first, second)
        place_in = region(home, row, half, part)
        source = own(half, part) if first == 0 and second == 0 else place_in
        at = 0 if way == 1 else 1
        if ring == 0:
            sems = (first_send.at[half, at, distance], first_recv.at[half, at, distance])
        else:
            index = (half, first % sizes[half][0], at, distance)
            sems = (second_send.at[index], second_recv.at[index])
        go(remote(source, place_in, *sems, neighbour(half, ring, way)))

    def receive(half, ring, first, second, way, distance):
        part = part_at(distance, way, sizes[half][ring])
        home, row = item(half, first, second)
        place_in = region(home, row, half, part)
        at = 0 if way == 1 else 1
        if ring == 0:
            sems = (first_send.at[half, at, distance], first_recv.at[half, at, distance])
        else:
            index = (half, first % sizes[half][0], at, distance)
            sems = (second_send.at[index], second_recv.at[index])
        remote(place_in, place_in, *sems, neighbour(half, ring, way)).wait_recv()

    twins = []

    def share(half, first, second):
        home, row = item(half, first, second)
        place_in = region(home, row, half, None)
        source = own(half, None) if first == 0 and second == 0 else place_in
        index = (half, first % sizes[half][0], second % sizes[half][1])
        go(remote(source, place_in, twin_send.at[index], twin_recv.at[index], twin))
        twins.append((half, first, second, index))

    def whole(half, first, second):
        if second == 0:
            for way in (1, -1):
                send(half, 1, first, 0, way, 1)
        share(half, first, second)

    def on_first(half, way, distance):
        size = sizes[half][0]
        receive(half, 0, way * distance, 0, way, distance)
        if (distance + 1) * 2 <= size:
            send(half, 0, way * distance, 0, way, distance + 1)
        if part_at(distance, way, size) is None or way == -1:
            whole(half, way * distance, 0)

    def on_second(half, first, way, distance):
        size = sizes[half][1]
        receive(half, 1, first, way * distance, way, distance)
        if (distance + 1) * 2 <= size:
            send(half, 1, first, way * distance, way, distance + 1)
        if part_at(distance, way, size) is None or way == -1:
            whole(half, first, way * distance)

    events = []
    for half in (0, 1):
        for way, distance, _ in arrivals(sizes[half][0]):
            events.append((distance, 0, half, 0, 0, way, distance))
        firsts = [(0, 0)]
        for way, distance, part in arrivals(sizes[half][0]):
            if part is None or way == -1:
                firsts.append((way * distance, distance))
        for first, ready in firsts:
            for way, distance, _ in arrivals(sizes[half][1]):
                events.append((ready + distance, 1, half, ready, first, way, distance))
    events.sort(key=lambda event: (event[0], event[1], event[3], event[6]))

    for half in (0, 1):
        for way in (1, -1):
            send(half, 0, 0, 0, way, 1)
    for half in (0, 1):
        whole(half, 0, 0)
    for k in range(1, sections):
        other = on_section((section + k) % sections)

        @pl.when(core == 0)
        def _():
            remote(
                down_ref, adapters.at[section, 0], adapter_send.at[k], adapter_recv.at[k], other
            ).start()

        @pl.when(core == 1)
        def _():
            remote(
                up_ref, adapters.at[section, 1], adapter_send.at[k], adapter_recv.at[k], other
            ).start()

    mine = pl.ds(pl.multiple_of(section * rows, rows), rows)
    cameras = camera_ref[mine, :]
    table = camera_table_ref[...].astype(jnp.float32)
    chosen = jnp.zeros((rows, width), jnp.float32)
    for view in range(table.shape[0]):
        chosen = jnp.where(cameras == view, table[view : view + 1, :], chosen)
    camera_rows[...] = chosen
    latent = latent_ref[mine, :].astype(jnp.float32)
    hidden_at[0, 0] = (latent + chosen).astype(jnp.bfloat16)
    step_table = step_table_ref[...].astype(jnp.float32)
    step_rows = lax.broadcasted_iota(jnp.int32, step_table.shape, 0)
    for step in range(2):
        picked = jnp.where(step_rows == steps_ref[step], step_table, 0.0)
        modulation[step] = 1.0 + jnp.sum(picked, axis=0, keepdims=True)

    for _, ring, half, _, first, way, distance in events:
        if ring == 0:
            on_first(half, way, distance)
        else:
            on_second(half, first, way, distance)

    for k in range(1, sections):
        behind = (section - k) % sections
        held = adapters.at[behind, core]
        remote(held, held, adapter_send.at[k], adapter_recv.at[k], on_section(behind)).wait()
        go(remote(held, held, adapter_send.at[sections + k], adapter_recv.at[sections + k], twin))
    for k in range(1, sections):
        behind = (section - k) % sections
        held = adapters.at[behind, 1 - core]
        index = sections + k
        remote(held, held, adapter_send.at[index], adapter_recv.at[index], twin).wait_recv()
    for copy, k in go_gain:
        copy.wait()
    for half, first, second, index in twins:
        home, row = item(half, first, second)
        columns = width // 2
        offset = pl.multiple_of((row * 2 + 1 - core) * block, block)
        held = weights.at[home, pl.ds(offset, block), pl.ds(half * columns, columns)]
        remote(held, held, twin_send.at[index], twin_recv.at[index], twin).wait_recv()
    for copy in local:
        copy.wait()
    for copy in pending:
        copy.wait_send()
    pending.clear()

    def normed_of(step, layer):
        hidden = hidden_at[step, layer].astype(jnp.float32)
        inverse = lax.rsqrt(jnp.mean(hidden * hidden, axis=-1, keepdims=True) + EPSILON)
        gain = gains[layer] * modulation[step]
        return hidden, inverse, gain, (hidden * inverse * gain).astype(jnp.bfloat16)

    def forward(step, layer):
        hidden, _, _, normed = normed_of(step, layer)
        low = lax.dot_general(
            normed, adapters[layer, 0], NT, preferred_element_type=jnp.float32
        ).astype(jnp.bfloat16)
        pre = jnp.dot(
            normed, weights[layer], preferred_element_type=jnp.float32
        ) + ADAPTER_SCALE * jnp.dot(low, adapters[layer, 1], preferred_element_type=jnp.float32)
        pre_at[step, layer] = pre
        low_at[step, layer] = low
        hidden_at[step, layer + 1] = (hidden + jax.nn.silu(pre)).astype(jnp.bfloat16)

    def forward_body(index, carry):
        step, layer = index // sections, index % sections
        forward(step, layer)

        @pl.when((step == 0) & (layer == sections - 1))
        def _():
            last = hidden_at[0, sections].astype(jnp.float32)
            first = latent_ref[mine, :].astype(jnp.float32)
            middle = (BLEND * (first + last)).astype(jnp.bfloat16)
            hidden_at[0, sections] = middle
            hidden_at[1, 0] = (middle.astype(jnp.float32) + camera_rows[...]).astype(jnp.bfloat16)

        return carry

    lax.fori_loop(0, 2 * sections, forward_body, 0)
    final = BLEND * (
        hidden_at[0, sections].astype(jnp.float32) + hidden_at[1, sections].astype(jnp.float32)
    )
    squashed = jnp.tanh(final)
    adjoint = (
        target_ref[mine, :].astype(jnp.float32) * (1.0 - squashed * squashed) * scale_factor
    )
    adjoint_at[...] = adjoint

    def backward(step, layer, gradient, earlier):
        hidden, inverse, gain, normed = normed_of(step, layer)
        pre = pre_at[step, layer]
        sigmoid = jax.nn.sigmoid(pre)
        pre_grad = (gradient * sigmoid * (1.0 + pre * (1.0 - sigmoid))).astype(jnp.bfloat16)
        low_grad = (
            ADAPTER_SCALE
            * lax.dot_general(
                pre_grad, adapters[layer, 1], NT, preferred_element_type=jnp.float32
            )
        ).astype(jnp.bfloat16)
        norm_grad = lax.dot_general(
            pre_grad, weights[layer], NT, preferred_element_type=jnp.float32
        ) + jnp.dot(low_grad, adapters[layer, 0], preferred_element_type=jnp.float32)
        down_term = lax.dot_general(normed, low_grad, TN, preferred_element_type=jnp.float32)
        up_term = ADAPTER_SCALE * lax.dot_general(
            pre_grad, low_at[step, layer], TN, preferred_element_type=jnp.float32
        )
        terms = jnp.concatenate([down_term, up_term], axis=1)
        terms = terms.reshape(depth_size, 2, block, 2 * rank)
        for side in range(2):
            total = terms[:, side]
            if earlier:
                total = total + pair_out[layer, side].astype(jnp.float32)
            pair_out[layer, side] = total.astype(jnp.bfloat16)
        scaled = hidden * inverse
        scaled_grad = norm_grad * gain
        result = gradient + inverse * (
            scaled_grad - scaled * jnp.mean(scaled_grad * scaled, axis=-1, keepdims=True)
        )
        return result.astype(jnp.bfloat16).astype(jnp.float32)

    def to_twin(layer):
        return remote(
            pair_out.at[layer, 1 - core],
            pair_in.at[layer],
            pair_sems.at[0, layer],
            pair_sems.at[1, layer],
            twin,
        )

    def to_depth(layer, k):
        other = (depth + k) % depth_size
        return remote(
            depth_out.at[layer, other],
            depth_in.at[layer, k - 1],
            depth_send.at[layer, k],
            depth_recv.at[layer, k],
            on_depth(other),
        )

    def pass_on(layer):
        to_twin(layer).wait_recv()
        total = pair_out[layer, core].astype(jnp.float32) + pair_in[layer].astype(jnp.float32)
        depth_out[layer] = total.astype(jnp.bfloat16)
        for k in range(1, depth_size):
            to_depth(layer, k).start()

    def late_body(index, gradient):
        layer = sections - 1 - index
        gradient = backward(1, layer, gradient, False)
        return gradient

    def early_body(index, gradient):
        layer = sections - 1 - index
        gradient = backward(0, layer, gradient, True)
        to_twin(layer).start()

        @pl.when(index > 0)
        def _():
            pass_on(layer + 1)

        return gradient

    gradient = lax.fori_loop(0, sections, late_body, BLEND * adjoint)
    gradient = BLEND * (BLEND * adjoint_at[...] + gradient)
    lax.fori_loop(0, sections, early_body, gradient)
    pass_on(0)

    def settle(layer, carry):
        total = depth_out[layer, depth].astype(jnp.float32)
        for k in range(1, depth_size):
            to_depth(layer, k).wait()
            total = total + depth_in[layer, k - 1].astype(jnp.float32)
        plane_out[layer] = total.astype(jnp.bfloat16)
        to_twin(layer).wait_send()
        return carry

    lax.fori_loop(0, sections, settle, 0)
    copies = []
    for k in range(1, sections):
        other = (section + k) % sections
        copy = remote(
            plane_out.at[other],
            plane_in.at[k - 1],
            plane_send.at[k],
            plane_recv.at[k],
            on_section(other),
        )
        copy.start()
        copies.append(copy)
    total = plane_out[section].astype(jnp.float32)
    for k, copy in enumerate(copies):
        copy.wait()
        total = total + plane_in[k].astype(jnp.float32)
    out_ref[...] = total


def local(
    latent,
    target,
    camera_of_token,
    timestep_indices,
    camera_embedding_table,
    timestep_embedding_table,
    layer_norm_gain,
    frozen_weight,
    adapter_down_weight,
    adapter_up_weight,
):
    sections, ways = lax.axis_size("section"), lax.axis_size("dp")
    width = latent.shape[1]
    rank = adapter_down_weight.shape[1]
    block = frozen_weight.shape[1]
    rows = latent.shape[0] // sections
    depth_size = ways // 2
    scale_factor = 1.0 / math.sqrt(latent.shape[0] * ways)
    longest = max(sections, depth_size)
    dma = pltpu.SemaphoreType.DMA
    bf16, f32 = jnp.bfloat16, jnp.float32
    vmem = pl.BlockSpec(memory_space=pltpu.VMEM)
    result = pl.pallas_call(
        functools.partial(kernel, sections, ways, scale_factor),
        out_shape=jax.ShapeDtypeStruct((block, 2 * rank), f32),
        in_specs=[pl.BlockSpec(memory_space=pltpu.SMEM)] + [vmem] * 9,
        out_specs=vmem,
        scratch_shapes=[
            pltpu.VMEM((sections, width, width), bf16),
            pltpu.VMEM((sections, 2, rank, width), bf16),
            pltpu.VMEM((sections, 1, width), f32),
            pltpu.VMEM((2, sections + 1, rows, width), bf16),
            pltpu.VMEM((2, sections, rows, width), f32),
            pltpu.VMEM((2, sections, rows, rank), bf16),
            pltpu.VMEM((2, 1, width), f32),
            pltpu.VMEM((rows, width), f32),
            pltpu.VMEM((rows, width), f32),
            pltpu.VMEM((sections, 2, depth_size, block, 2 * rank), bf16),
            pltpu.VMEM((sections, depth_size, block, 2 * rank), bf16),
            pltpu.VMEM((sections, depth_size, block, 2 * rank), bf16),
            pltpu.VMEM((sections, depth_size - 1, block, 2 * rank), bf16),
            pltpu.VMEM((sections, block, 2 * rank), bf16),
            pltpu.VMEM((sections - 1, block, 2 * rank), bf16),
            dma((4,)),
            dma((2, 2, longest // 2 + 1)),
            dma((2, 2, longest // 2 + 1)),
            dma((2, longest, 2, longest // 2 + 1)),
            dma((2, longest, 2, longest // 2 + 1)),
            dma((2, longest, longest)),
            dma((2, longest, longest)),
            dma((sections,)),
            dma((sections,)),
            dma((2 * sections,)),
            dma((2 * sections,)),
            dma((2, sections)),
            dma((sections, depth_size)),
            dma((sections, depth_size)),
            dma((sections,)),
            dma((sections,)),
        ],
        compiler_params=pltpu.CompilerParams(
            collective_id=0, has_side_effects=True, vmem_limit_bytes=66 * 1024 * 1024 - 2 * 1024 * 1024 - 65536
        ),
    )(
        timestep_indices,
        latent,
        target,
        camera_of_token[:, None],
        camera_embedding_table,
        timestep_embedding_table,
        layer_norm_gain,
        frozen_weight[0],
        adapter_down_weight[0],
        adapter_up_weight[0],
    )
    turned = result.T
    return (turned[None, :rank], turned[None, rank:])


def solution(mesh):
    in_specs = (
        P("dp", None),
        P("dp", None),
        P("dp"),
        P(),
        P(),
        P(),
        P("section", None),
        P("section", "dp", None),
        P("section", None, None),
        P("section", None, None),
    )
    out_specs = (P("section", None, "dp"), P("section", None, "dp"))
    return jax.shard_map(local, mesh=mesh, in_specs=in_specs, out_specs=out_specs, check_vma=False)
```

time: 375 us -> 164 us (0.44)
  waiting for transfers between devices: 290 us -> 0 us
  Pallas kernels: 0 us -> 159 us
  matrix products: 46.6 us -> 0 us
  between operations: 14.3 us -> 0.65 us
  blocking collectives: 9.8 us -> 0 us
  other arithmetic: 5.8 us -> 0 us
  local copies, waits for them, and re-layouts: 7.99 us -> 3.93 us
    pallas_call x0 -> x1, Pallas kernels: none -> 159 us  [local(): pl.pallas_call(functools.partial(kernel, sections, ways, scale_factor), o...]
    all_gather x2 -> x0, waiting for transfers between devices: 146 us -> none  [the longest x1 126 us: local(): lax.all_gather(frozen_weight[0], ('section', 'dp'), axis=0, tiled=True)]
    reduce_scatter x1 -> x0, waiting for transfers between devices: 142 us -> none  [local(): lax.psum_scatter(sums, ('section', 'dp'), scatter_dimension=0, tiled=True)]
    dot_general x63 -> x0, matrix products: 46.6 us -> none  [the longest x8 15.9 us: forward_layer_pass(): jnp.dot(normalized_hidden, layer_weight, preferred_element_type=jnp.float32)]
    all_gather x1 -> x0, blocking collectives: 9.8 us -> none  [local(): gains = lax.all_gather(layer_norm_gain, 'section', axis=0, tiled=True)]
  transfers between devices with their start and end apart: 3 -> 0, of which waited for: 3 -> 0; matrix products, arithmetic and copies ran while one was open for 1% -> 0% of each run, Pallas kernels for 0% -> 0%
where the time goes in v2:
time: 164 us
  Pallas kernels  159 us (97%)
  local copies, waits for them, and re-layouts  3.93 us (2%)
    pallas_call x1, Pallas kernels, local(): pl.pallas_call(functools.partial(kernel, sections, ways, scale_factor), o...  159 us

profile of v2, /device:TPU:0, one launch (start us, length us, event | category | flops | bytes accessed | tf_op | source)
XLA Modules:
  0.0 164.1 jit_solution(5191798204114899249)
XLA Ops:
  0.6 0.0 copy-start
  0.6 0.7 copy-done
  1.3 0.8 copy.14.camera_ref
  2.1 159.5 %shard_map.113 = f32[192,128]{1,0:T(8,128)} custom-call(s32[2]{0:T(128)} %steps_ref.1, bf16[256,1536]{1,0:T(8,128)(2,1)} %latent_ref.1, bf16[256,1536]{1,0:T(8,128)(2,1)} %target_ref.1, s32[256,1]{1,0:T(8,128)} %copy.14.camera_ref, bf16[6,1536]{1,0:T(8,128)(2,1)} %camera_table_ref.1, bf16[50,1536]{1,0:T(8,128)(2,1)} %step_table_ref.1, f32[1,1536]{1,0:T(1,128)} %gain_ref.1, ...), custom_call_target="tpu_custom_call" | custom-call | tf_op jit(solution)/shard_map/pallas_call | solution.py:507
  161.6 1.1 slice_bitcast_fusion
  162.6 0.7 copy.16
  163.4 0.7 copy.15
Async XLA Ops:
  0.6 0.7 copy-start

commit v3 on v2

--- a/solution.py
+++ b/solution.py
@@ -151,22 +151,22 @@
         copy.start()
         go_gain.append((copy, k))
 
-    def region(home, row, half, part):
-        columns = width // 2
-        start = half * columns
+    tiles = width // 128
+    cut = max(tiles // 4, 1)
+
+    def columns_of(half, part):
+        start, stop = (0, cut) if half == 0 else (cut, tiles)
+        middle = (start + stop) // 2
         if part is not None:
-            columns = columns // 2
-            start = start + part * columns
-        offset = pl.multiple_of((row * 2 + core) * block, block)
-        return weights.at[home, pl.ds(offset, block), pl.ds(start, columns)]
+            start, stop = (start, middle) if part == 0 else (middle, stop)
+        return pl.ds(start * 128, (stop - start) * 128)
+
+    def region(home, row, half, part, side=core):
+        offset = pl.multiple_of((row * 2 + side) * block, block)
+        return weights.at[home, pl.ds(offset, block), columns_of(half, part)]
 
     def own(half, part):
-        columns = width // 2
-        start = half * columns
-        if part is not None:
-            columns = columns // 2
-            start = start + part * columns
-        return shard_ref.at[:, pl.ds(start, columns)]
+        return shard_ref.at[:, columns_of(half, part)]
 
     local = [
         pltpu.make_async_copy(
@@ -321,9 +321,7 @@
         copy.wait()
     for half, first, second, index in twins:
         home, row = item(half, first, second)
-        columns = width // 2
-        offset = pl.multiple_of((row * 2 + 1 - core) * block, block)
-        held = weights.at[home, pl.ds(offset, block), pl.ds(half * columns, columns)]
+        held = region(home, row, half, None, 1 - core)
         remote(held, held, twin_send.at[index], twin_recv.at[index], twin).wait_recv()
     for copy in local:
         copy.wait()

time: 164 us -> 142 us (0.87)
  Pallas kernels: 159 us -> 137 us
    pallas_call x1, Pallas kernels: 159 us -> 137 us  [local(): pl.pallas_call(functools.partial(kernel, sections, ways, scale_factor), o...]
where the time goes in v3:
time: 142 us
  Pallas kernels  137 us (96%)
  local copies, waits for them, and re-layouts  3.93 us (3%)
    pallas_call x1, Pallas kernels, local(): pl.pallas_call(functools.partial(kernel, sections, ways, scale_factor), o...  137 us

profile of v3, /device:TPU:0, one launch (start us, length us, event | category | flops | bytes accessed | tf_op | source)
XLA Modules:
  0.0 142.1 jit_solution(8522670947726648955)
XLA Ops:
  0.6 0.0 copy-start
  0.6 0.7 copy-done
  1.3 0.8 copy.14.camera_ref
  2.1 137.5 %shard_map.113 = f32[192,128]{1,0:T(8,128)} custom-call(s32[2]{0:T(128)} %steps_ref.1, bf16[256,1536]{1,0:T(8,128)(2,1)} %latent_ref.1, bf16[256,1536]{1,0:T(8,128)(2,1)} %target_ref.1, s32[256,1]{1,0:T(8,128)} %copy.14.camera_ref, bf16[6,1536]{1,0:T(8,128)(2,1)} %camera_table_ref.1, bf16[50,1536]{1,0:T(8,128)(2,1)} %step_table_ref.1, f32[1,1536]{1,0:T(1,128)} %gain_ref.1, ...), custom_call_target="tpu_custom_call" | custom-call | tf_op jit(solution)/shard_map/pallas_call | solution.py:505
  139.6 1.1 slice_bitcast_fusion
  140.6 0.7 copy.16
  141.4 0.7 copy.15
Async XLA Ops:
  0.6 0.7 copy-start

commit v4 on v3

--- a/solution.py
+++ b/solution.py
@@ -72,7 +72,8 @@
     shard_ref,
     down_ref,
     up_ref,
-    out_ref,
+    down_out_ref,
+    up_out_ref,
     weights,
     adapters,
     gains,
@@ -301,17 +302,23 @@
         picked = jnp.where(step_rows == steps_ref[step], step_table, 0.0)
         modulation[step] = 1.0 + jnp.sum(picked, axis=0, keepdims=True)
 
-    for _, ring, half, _, first, way, distance in events:
+    def hand_adapters():
+        for k in range(1, sections):
+            behind = (section - k) % sections
+            held = adapters.at[behind, core]
+            remote(held, held, adapter_send.at[k], adapter_recv.at[k], on_section(behind)).wait()
+            go(remote(held, held, adapter_send.at[sections + k], adapter_recv.at[sections + k], twin))
+
+    handed = False
+    for level, ring, half, _, first, way, distance in events:
+        if level > 1 and not handed:
+            hand_adapters()
+            handed = True
         if ring == 0:
             on_first(half, way, distance)
         else:
             on_second(half, first, way, distance)
 
-    for k in range(1, sections):
-        behind = (section - k) % sections
-        held = adapters.at[behind, core]
-        remote(held, held, adapter_send.at[k], adapter_recv.at[k], on_section(behind)).wait()
-        go(remote(held, held, adapter_send.at[sections + k], adapter_recv.at[sections + k], twin))
     for k in range(1, sections):
         behind = (section - k) % sections
         held = adapters.at[behind, 1 - core]
@@ -325,9 +332,6 @@
         remote(held, held, twin_send.at[index], twin_recv.at[index], twin).wait_recv()
     for copy in local:
         copy.wait()
-    for copy in pending:
-        copy.wait_send()
-    pending.clear()
 
     def normed_of(step, layer):
         hidden = hidden_at[step, layer].astype(jnp.float32)
@@ -450,33 +454,41 @@
     lax.fori_loop(0, sections, early_body, gradient)
     pass_on(0)
 
-    def settle(layer, carry):
+    def to_section(layer):
+        k = (layer - section) % sections
+        return remote(
+            plane_out.at[layer],
+            plane_in.at[k - 1],
+            plane_send.at[k],
+            plane_recv.at[k],
+            on_section(layer),
+        )
+
+    def settle(index, carry):
+        layer = sections - 1 - index
         total = depth_out[layer, depth].astype(jnp.float32)
         for k in range(1, depth_size):
             to_depth(layer, k).wait()
             total = total + depth_in[layer, k - 1].astype(jnp.float32)
         plane_out[layer] = total.astype(jnp.bfloat16)
+
+        @pl.when(layer != section)
+        def _():
+            to_section(layer).start()
+
         to_twin(layer).wait_send()
         return carry
 
     lax.fori_loop(0, sections, settle, 0)
-    copies = []
+    total = plane_out[section].astype(jnp.float32)
     for k in range(1, sections):
-        other = (section + k) % sections
-        copy = remote(
-            plane_out.at[other],
-            plane_in.at[k - 1],
-            plane_send.at[k],
-            plane_recv.at[k],
-            on_section(other),
-        )
-        copy.start()
-        copies.append(copy)
-    total = plane_out[section].astype(jnp.float32)
-    for k, copy in enumerate(copies):
-        copy.wait()
-        total = total + plane_in[k].astype(jnp.float32)
-    out_ref[...] = total
+        to_section((section + k) % sections).wait()
+        total = total + plane_in[k - 1].astype(jnp.float32)
+    for copy in pending:
+        copy.wait_send()
+    turned = total.T
+    down_out_ref[...] = turned[:rank]
+    up_out_ref[...] = turned[rank:]
 
 
 def local(
@@ -504,9 +516,9 @@
     vmem = pl.BlockSpec(memory_space=pltpu.VMEM)
     result = pl.pallas_call(
         functools.partial(kernel, sections, ways, scale_factor),
-        out_shape=jax.ShapeDtypeStruct((block, 2 * rank), f32),
+        out_shape=[jax.ShapeDtypeStruct((rank, block), f32)] * 2,
         in_specs=[pl.BlockSpec(memory_space=pltpu.SMEM)] + [vmem] * 9,
-        out_specs=vmem,
+        out_specs=[vmem] * 2,
         scratch_shapes=[
             pltpu.VMEM((sections, width, width), bf16),
             pltpu.VMEM((sections, 2, rank, width), bf16),
@@ -555,8 +567,7 @@
         adapter_down_weight[0],
         adapter_up_weight[0],
     )
-    turned = result.T
-    return (turned[None, :rank], turned[None, rank:])
+    return (result[0][None], result[1][None])
 
 
 def solution(mesh):

time: 142 us -> 139 us (0.979)
  Pallas kernels: 137 us -> 135 us
    pallas_call x1, Pallas kernels: 137 us -> 135 us  [local(): pl.pallas_call(functools.partial(kernel, sections, ways, scale_factor), o...]
where the time goes in v4:
time: 139 us
  Pallas kernels  135 us (97%)
  local copies, waits for them, and re-layouts  3.6 us (3%)
    pallas_call x1, Pallas kernels, local(): pl.pallas_call(functools.partial(kernel, sections, ways, scale_factor), o...  135 us
    unnamed x6, local copies, waits for them, and re-layouts  2.81 us

profile of v4, /device:TPU:0, one launch (start us, length us, event | category | flops | bytes accessed | tf_op | source)
XLA Modules:
  0.0 138.9 jit_solution(4156491543516248520)
XLA Ops:
  0.6 0.0 copy-start.1
  0.6 0.7 copy-done.1
  1.3 0.8 copy.12.camera_ref
  2.1 134.6 %shard_map.113 = (f32[64,192]{1,0:T(8,128)}, f32[64,192]{1,0:T(8,128)}) custom-call(s32[2]{0:T(128)} %steps_ref.1, bf16[256,1536]{1,0:T(8,128)(2,1)} %latent_ref.1, bf16[256,1536]{1,0:T(8,128)(2,1)} %target_ref.1, s32[256,1]{1,0:T(8,128)} %copy.12.camera_ref, bf16[6,1536]{1,0:T(8,128)(2,1)} %camera_table_ref.1, bf16[50,1536]{1,0:T(8,128)(2,1)} %step_table_ref.1, ...), custom_call_target="tpu_custom_call" | custom-call | tf_op jit(solution)/shard_map/pallas_call | solution.py:517
  136.7 0.0 copy-start
  136.7 1.5 %copy.15 = f32[1,64,192]{2,1,0:T(8,128)} copy(f32[1,64,192]{2,1,0:T(8,128)} %bitcast.10) | data formatting | bytes 98304
  138.3 0.0 copy-done
  138.3 0.6 copy.16
Async XLA Ops:
  0.6 0.7 copy-start.1
  136.7 1.5 %copy-start = (f32[64,192]{1,0:T(8,128)S(1)}, f32[64,192]{1,0:T(8,128)}, u32[]{:S(2)}) copy-start(f32[64,192]{1,0:T(8,128)} %get-tuple-element.5) | copy-start | bytes 147460
